TPU v7x, 32 devices: a whole 2x2x4 slice. The times are simulated.
32 devices in a mesh: fsdp: 8 (over z, x), rep: 4 (over y, core).
Axes of the slice: x: 2, y: 2, z: 4, core: 2. Of those that a mesh axis runs over, the one named last changes fastest.
Arguments:
- latents: float32 [256, 256, 384], P(('fsdp', 'rep')), may hold values from -6 to 6
- condition: float32 [256, 384], P(('fsdp', 'rep')), may hold values from -6 to 6
- cotangent: float32 [256, 256, 384], P(('fsdp', 'rep')), may hold values from -6 to 6
- w_ada: bfloat16 [2, 384, 2304], P(None, 'fsdp'), may hold values from -0.3125 to 0.3125
- b_ada: bfloat16 [2, 2304], P(None, 'fsdp'), may hold values from -3 to 3
- w_qkv: bfloat16 [2, 384, 1152], P(None, 'fsdp'), may hold values from -0.3125 to 0.3125
- qv_bias: bfloat16 [2, 768], P(None, 'fsdp'), may hold values from -3 to 3
- w_out: bfloat16 [2, 384, 384], P(None, 'fsdp'), may hold values from -1.25 to 1.25
- b_out: bfloat16 [2, 384], P(None, 'fsdp'), may hold values from -3 to 3
- w_up: bfloat16 [2, 384, 1536], P(None, 'fsdp'), may hold values from -0.3125 to 0.3125
- b_up: bfloat16 [2, 1536], P(None, 'fsdp'), may hold values from -3 to 3
- w_down: bfloat16 [2, 1536, 384], P(None, 'fsdp'), may hold values from -0.15625 to 0.15625
- b_down: bfloat16 [2, 384], P(None, 'fsdp'), may hold values from -3 to 3
Outputs:
- output: float32 [256, 256, 384], P(('fsdp', 'rep'))
- grad_latents: float32 [256, 256, 384], P(('fsdp', 'rep'))
- grad_condition: float32 [256, 384], P(('fsdp', 'rep'))
- grad_w_ada: float32 [2, 384, 2304], P(None, 'fsdp')
- grad_b_ada: float32 [2, 2304], P(None, 'fsdp')
- grad_w_qkv: float32 [2, 384, 1152], P(None, 'fsdp')
- grad_qv_bias: float32 [2, 768], P(None, 'fsdp')
- grad_w_out: float32 [2, 384, 384], P(None, 'fsdp')
- grad_b_out: float32 [2, 384], P(None, 'fsdp')
- grad_w_up: float32 [2, 384, 1536], P(None, 'fsdp')
- grad_b_up: float32 [2, 1536], P(None, 'fsdp')
- grad_w_down: float32 [2, 1536, 384], P(None, 'fsdp')
- grad_b_down: float32 [2, 384], P(None, 'fsdp')
All inputs are finite; a program needn't handle non-finite values.
Results may differ from a plain program's by a relative error of at most 0.029.
The roundings to bfloat16 on the way count: a program that leaves them out, or rounds other values in their place, can miss the bound.
Values may be sent and summed in bfloat16 or wider, within the bound.
No kernel may reach another device: no remote copies, remote signals or barrier semaphores. Data moves between devices by JAX's collectives and lax.ppermute only.
A program may use at most 320 MiB of HBM per device.

v0:
```python
import jax
import jax.numpy as jnp
from jax import lax
from jax.sharding import PartitionSpec as P

LAYERS = 2
GELU_C = 0.7978845608028654
GELU_A = 0.044715
EPS = 1e-06


def as_sent(shard):

    def short(part):
        return part.astype(jnp.bfloat16) if part.dtype == jnp.float32 else part

    return jax.tree.map(short, shard)


def pair_product(form, left, right):
    return jnp.einsum(form, left, right, preferred_element_type=jnp.float32)


def matmul(inputs, weight):
    flattened = inputs.reshape(-1, inputs.shape[-1])
    result = jnp.dot(flattened, weight, preferred_element_type=jnp.float32)
    return result.reshape(inputs.shape[:-1] + (weight.shape[-1],))


def matmul_back(grads, weight):
    flattened = grads.reshape(-1, grads.shape[-1])
    result = lax.dot_general(
        flattened, weight, (((1,), (1,)), ((), ())), preferred_element_type=jnp.float32
    )
    return result.reshape(grads.shape[:-1] + (weight.shape[0],))


def outer_sum(left, right):
    return lax.dot_general(
        left.reshape(-1, left.shape[-1]),
        right.reshape(-1, right.shape[-1]),
        (((0,), (0,)), ((), ())),
        preferred_element_type=jnp.float32,
    )


def norm_rows(stream):
    centered = stream - jnp.mean(stream, axis=-1, keepdims=True)
    inverse = lax.rsqrt(jnp.mean(centered * centered, axis=-1, keepdims=True) + EPS)
    return (centered * inverse, inverse)


def norm_back(grad_normed, normed, inverse):
    return inverse * (
        grad_normed
        - jnp.mean(grad_normed, axis=-1, keepdims=True)
        - normed * jnp.mean(grad_normed * normed, axis=-1, keepdims=True)
    )


def gelu_parts(pre_act):
    tanh_part = jnp.tanh(GELU_C * (pre_act + GELU_A * pre_act * pre_act * pre_act))
    value_part = 0.5 * pre_act * (1.0 + tanh_part)
    slope_part = 0.5 * (1.0 + tanh_part) + 0.5 * pre_act * (
        1.0 - tanh_part * tanh_part
    ) * GELU_C * (1.0 + 3.0 * GELU_A * pre_act * pre_act)
    return (value_part, slope_part)


def forward_pieces(stream, cond_rows, params):
    w_ada, b_ada, w_qkv, qv_bias, w_out, b_out, w_up, b_up, w_down, b_down = params
    model_width = stream.shape[-1]
    head_count = model_width // 64
    silu_cond = jax.nn.silu(cond_rows).astype(jnp.bfloat16)
    modulation = jnp.dot(silu_cond, w_ada, preferred_element_type=jnp.float32) + b_ada.astype(
        jnp.float32
    )
    pieces = [modulation[:, None, i * model_width : (i + 1) * model_width] for i in range(6)]
    shift1, scale1, gate1, shift2, scale2, gate2 = pieces
    normed1, inverse1 = norm_rows(stream)
    attn_in = (normed1 * (1.0 + scale1) + shift1).astype(jnp.bfloat16)
    bias_query = qv_bias[:model_width].astype(jnp.float32)
    bias_value = qv_bias[model_width:].astype(jnp.float32)
    full_bias = jnp.concatenate([bias_query, jnp.zeros_like(bias_query), bias_value])
    projected = (matmul(attn_in, w_qkv) + full_bias).astype(jnp.bfloat16)
    head_shape = stream.shape[:2] + (head_count, 64)
    query = projected[..., :model_width].reshape(head_shape)
    key_heads = projected[..., model_width : 2 * model_width].reshape(head_shape)
    value_heads = projected[..., 2 * model_width :].reshape(head_shape)
    scores = pair_product("bqhe,bkhe->bhqk", query, key_heads) * 0.125
    log_total = jax.nn.logsumexp(scores, axis=-1, keepdims=True)
    attention = jnp.exp(scores - log_total)
    attention_b = attention.astype(jnp.bfloat16)
    attended = (
        pair_product("bhqk,bkhe->bqhe", attention_b, value_heads)
        .astype(jnp.bfloat16)
        .reshape(stream.shape)
    )
    branch = matmul(attended, w_out) + b_out.astype(jnp.float32)
    middle = stream + gate1 * branch
    normed2, inverse2 = norm_rows(middle)
    mlp_in = (normed2 * (1.0 + scale2) + shift2).astype(jnp.bfloat16)
    hidden_pre = matmul(mlp_in, w_up) + b_up.astype(jnp.float32)
    activated_f, slope = gelu_parts(hidden_pre)
    activated = activated_f.astype(jnp.bfloat16)
    mlp_out = matmul(activated, w_down) + b_down.astype(jnp.float32)
    result = middle + gate2 * mlp_out
    saved = (
        silu_cond,
        pieces,
        normed1,
        inverse1,
        attn_in,
        query,
        key_heads,
        value_heads,
        attention,
        attention_b,
        attended,
        branch,
        normed2,
        inverse2,
        mlp_in,
        slope,
        activated,
        mlp_out,
    )
    return (result, saved)


def layer_forward(stream, cond_rows, params):
    return forward_pieces(stream, cond_rows, params)[0]


def layer_grads(stream, cond_rows, params, grad_result):
    w_ada, b_ada, w_qkv, qv_bias, w_out, b_out, w_up, b_up, w_down, b_down = params
    result, saved = forward_pieces(stream, cond_rows, params)
    (
        silu_cond,
        pieces,
        normed1,
        inverse1,
        attn_in,
        query,
        key_heads,
        value_heads,
        attention,
        attention_b,
        attended,
        branch,
        normed2,
        inverse2,
        mlp_in,
        slope,
        activated,
        mlp_out,
    ) = saved
    shift1, scale1, gate1, shift2, scale2, gate2 = pieces
    grad_z = gate2 * grad_result
    grad_z_b = grad_z.astype(jnp.bfloat16)
    grad_gate2 = jnp.sum(grad_result * mlp_out, axis=1)
    grad_b_down = jnp.sum(grad_z, axis=(0, 1))
    grad_w_down = outer_sum(activated, grad_z_b)
    grad_pre = matmul_back(grad_z_b, w_down) * slope
    grad_pre_b = grad_pre.astype(jnp.bfloat16)
    grad_b_up = jnp.sum(grad_pre, axis=(0, 1))
    grad_w_up = outer_sum(mlp_in, grad_pre_b)
    grad_mlp_in = matmul_back(grad_pre_b, w_up)
    grad_scale2 = jnp.sum(grad_mlp_in * normed2, axis=1)
    grad_shift2 = jnp.sum(grad_mlp_in, axis=1)
    grad_middle = grad_result + norm_back(grad_mlp_in * (1.0 + scale2), normed2, inverse2)
    grad_branch = gate1 * grad_middle
    grad_branch_b = grad_branch.astype(jnp.bfloat16)
    grad_gate1 = jnp.sum(grad_middle * branch, axis=1)
    grad_b_out = jnp.sum(grad_branch, axis=(0, 1))
    grad_w_out = outer_sum(attended, grad_branch_b)
    grad_attended = matmul_back(grad_branch_b, w_out).astype(jnp.bfloat16).reshape(query.shape)
    grad_value = pair_product("bhqk,bqhe->bkhe", attention_b, grad_attended)
    grad_probs = pair_product("bqhe,bkhe->bhqk", grad_attended, value_heads)
    row_dot = jnp.sum(attention * grad_probs, axis=-1, keepdims=True)
    grad_scores = (attention * (grad_probs - row_dot) * 0.125).astype(jnp.bfloat16)
    grad_query = pair_product("bhqk,bkhe->bqhe", grad_scores, key_heads)
    grad_key = pair_product("bhqk,bqhe->bkhe", grad_scores, query)
    flat_shape = stream.shape
    grad_proj = jnp.concatenate(
        [
            grad_query.reshape(flat_shape),
            grad_key.reshape(flat_shape),
            grad_value.reshape(flat_shape),
        ],
        axis=-1,
    )
    grad_proj_b = grad_proj.astype(jnp.bfloat16)
    grad_qv_bias = jnp.concatenate(
        [
            jnp.sum(grad_query.reshape(flat_shape), axis=(0, 1)),
            jnp.sum(grad_value.reshape(flat_shape), axis=(0, 1)),
        ]
    )
    grad_w_qkv = outer_sum(attn_in, grad_proj_b)
    grad_attn_in = matmul_back(grad_proj_b, w_qkv)
    grad_scale1 = jnp.sum(grad_attn_in * normed1, axis=1)
    grad_shift1 = jnp.sum(grad_attn_in, axis=1)
    grad_stream = grad_middle + norm_back(grad_attn_in * (1.0 + scale1), normed1, inverse1)
    grad_mod = jnp.concatenate(
        [grad_shift1, grad_scale1, grad_gate1, grad_shift2, grad_scale2, grad_gate2], axis=-1
    )
    grad_w_ada = jnp.dot(silu_cond.astype(jnp.float32).T, grad_mod, precision=lax.Precision.HIGHEST)
    grad_b_ada = jnp.sum(grad_mod, axis=0)
    grad_silu = jnp.dot(grad_mod, w_ada.astype(jnp.float32).T, precision=lax.Precision.HIGHEST)
    sigmoid_c = jax.nn.sigmoid(cond_rows)
    grad_cond = grad_silu * sigmoid_c * (1.0 + cond_rows * (1.0 - sigmoid_c))
    gradients = (
        grad_w_ada,
        grad_b_ada,
        grad_w_qkv,
        grad_qv_bias,
        grad_w_out,
        grad_b_out,
        grad_w_up,
        grad_b_up,
        grad_w_down,
        grad_b_down,
    )
    return (grad_stream, grad_cond, gradients)


def body(
    latents,
    condition,
    cotangent,
    w_ada,
    b_ada,
    w_qkv,
    qv_bias,
    w_out,
    b_out,
    w_up,
    b_up,
    w_down,
    b_down,
):
    stacked = (w_ada, b_ada, w_qkv, qv_bias, w_out, b_out, w_up, b_up, w_down, b_down)
    inputs = []
    kept_weights = []
    stream = latents
    for layer_index in range(LAYERS):
        owned_rows = tuple((weight[layer_index] for weight in stacked))
        params = jax.tree.map(
            lambda part, own: part.astype(own.dtype),
            lax.all_gather(as_sent(owned_rows), "fsdp", axis=0, tiled=True),
            owned_rows,
        )
        kept_weights.append(params)
        inputs.append(stream)
        stream = layer_forward(stream, condition, params)
    grad_stream = cotangent
    grad_cond = jnp.zeros(condition.shape, jnp.float32)
    shards = [None] * LAYERS
    for layer_index in reversed(range(LAYERS)):
        owned_rows = tuple((weight[layer_index] for weight in stacked))
        params = jax.tree.map(
            lambda part, own: part.astype(own.dtype),
            lax.all_gather(as_sent(owned_rows), "fsdp", axis=0, tiled=True),
            owned_rows,
        )
        grad_stream, cond_part, gradients = layer_grads(
            inputs[layer_index], condition, params, grad_stream
        )
        grad_cond = grad_cond + cond_part
        owned_sums = (
            lax.psum_scatter(
                gradients[0].astype(jnp.bfloat16), "fsdp", scatter_dimension=0, tiled=True
            ).astype(jnp.float32),
            lax.psum_scatter(
                gradients[1].astype(jnp.bfloat16), "fsdp", scatter_dimension=0, tiled=True
            ).astype(jnp.float32),
            lax.psum_scatter(
                gradients[2].astype(jnp.bfloat16), "fsdp", scatter_dimension=0, tiled=True
            ).astype(jnp.float32),
            lax.psum_scatter(
                gradients[3].astype(jnp.bfloat16), "fsdp", scatter_dimension=0, tiled=True
            ).astype(jnp.float32),
            lax.psum_scatter(
                gradients[4].astype(jnp.bfloat16), "fsdp", scatter_dimension=0, tiled=True
            ).astype(jnp.float32),
            lax.psum_scatter(
                gradients[5].astype(jnp.bfloat16), "fsdp", scatter_dimension=0, tiled=True
            ).astype(jnp.float32),
            lax.psum_scatter(
                gradients[6].astype(jnp.bfloat16), "fsdp", scatter_dimension=0, tiled=True
            ).astype(jnp.float32),
            lax.psum_scatter(
                gradients[7].astype(jnp.bfloat16), "fsdp", scatter_dimension=0, tiled=True
            ).astype(jnp.float32),
            lax.psum_scatter(
                gradients[8].astype(jnp.bfloat16), "fsdp", scatter_dimension=0, tiled=True
            ).astype(jnp.float32),
            lax.psum_scatter(
                gradients[9].astype(jnp.bfloat16), "fsdp", scatter_dimension=0, tiled=True
            ).astype(jnp.float32),
        )
        owned_sums = (
            lax.psum(owned_sums[0].astype(jnp.bfloat16), "rep").astype(jnp.float32),
            lax.psum(owned_sums[1].astype(jnp.bfloat16), "rep").astype(jnp.float32),
            lax.psum(owned_sums[2].astype(jnp.bfloat16), "rep").astype(jnp.float32),
            lax.psum(owned_sums[3].astype(jnp.bfloat16), "rep").astype(jnp.float32),
            lax.psum(owned_sums[4].astype(jnp.bfloat16), "rep").astype(jnp.float32),
            lax.psum(owned_sums[5].astype(jnp.bfloat16), "rep").astype(jnp.float32),
            lax.psum(owned_sums[6].astype(jnp.bfloat16), "rep").astype(jnp.float32),
            lax.psum(owned_sums[7].astype(jnp.bfloat16), "rep").astype(jnp.float32),
            lax.psum(owned_sums[8].astype(jnp.bfloat16), "rep").astype(jnp.float32),
            lax.psum(owned_sums[9].astype(jnp.bfloat16), "rep").astype(jnp.float32),
        )
        shards[layer_index] = owned_sums
    stacked_grads = tuple((jnp.stack([shards[j][i] for j in range(LAYERS)]) for i in range(10)))
    return (stream, grad_stream, grad_cond) + stacked_grads


def solution(mesh):
    in_specs = (
        P(("fsdp", "rep"), None, None),
        P(("fsdp", "rep"), None),
        P(("fsdp", "rep"), None, None),
        P(None, "fsdp", None),
        P(None, "fsdp"),
        P(None, "fsdp", None),
        P(None, "fsdp"),
        P(None, "fsdp", None),
        P(None, "fsdp"),
        P(None, "fsdp", None),
        P(None, "fsdp"),
        P(None, "fsdp", None),
        P(None, "fsdp"),
    )
    out_specs = (
        P(("fsdp", "rep"), None, None),
        P(("fsdp", "rep"), None, None),
        P(("fsdp", "rep"), None),
        P(None, "fsdp", None),
        P(None, "fsdp"),
        P(None, "fsdp", None),
        P(None, "fsdp"),
        P(None, "fsdp", None),
        P(None, "fsdp"),
        P(None, "fsdp", None),
        P(None, "fsdp"),
        P(None, "fsdp", None),
        P(None, "fsdp"),
    )
    return jax.shard_map(body, mesh=mesh, in_specs=in_specs, out_specs=out_specs, check_vma=False)
```

profile of v0, /device:TPU:0, one launch (start us, length us, event | category | flops | bytes accessed | tf_op | source)
XLA Modules:
  0.0 1179.6 jit_solution(6326753263943865538)
XLA Ops:
  20.5 39.6 %all-reduce.21 = (bf16[768]{0:T(1024)(128)(2,1)S(1)}, bf16[2304]{0:T(1024)(128)(2,1)S(1)}, bf16[384]{0:T(512)(128)(2,1)S(1)}, bf16[1536]{0:T(1024)(128)(2,1)S(1)...) all-reduce(bf16[768]{0:T(1024)(128)(2,1)S(1)} %dynamic-update-slice, ...), channel_id=5, replica_groups=mesh['fsdp'=8,'rep'=4] {'fsdp'}, use_global_device_ids=true, to_apply=%add.1 | all-reduce | flops 10752 | bytes 43008
  66.5 33.9 %all-gather.14 = bf16[1,384,384]{2,1,0:T(8,128)(2,1)} all-gather(bf16[1,48,384]{2,1,0:T(8,128)(2,1)S(1)} %get-tuple-element.118), channel_id=16, replica_groups=mesh['fsdp'=8,'rep'=4] {'fsdp'}, dimensions={1}, use_global_device_ids=true | all-gather | bytes 331776 | tf_op jit(solution)/shard_map/all_gather | solution.py:251
  100.4 31.4 %all-gather.4 = bf16[1,384,384]{2,1,0:T(8,128)(2,1)S(1)} all-gather(bf16[1,48,384]{2,1,0:T(8,128)(2,1)S(1)} %get-tuple-element.119), channel_id=6, replica_groups=mesh['fsdp'=8,'rep'=4] {'fsdp'}, dimensions={1}, use_global_device_ids=true | all-gather | bytes 331776 | tf_op jit(solution)/shard_map/all_gather | solution.py:251
  131.8 35.8 %all-gather.12 = bf16[1,384,1152]{2,1,0:T(8,128)(2,1)} all-gather(bf16[1,48,1152]{2,1,0:T(8,128)(2,1)S(1)} %get-tuple-element.110), channel_id=14, replica_groups=mesh['fsdp'=8,'rep'=4] {'fsdp'}, dimensions={1}, use_global_device_ids=true | all-gather | bytes 995328 | tf_op jit(solution)/shard_map/all_gather | solution.py:251
  167.6 35.7 %all-gather.2 = bf16[1,384,1152]{2,1,0:T(8,128)(2,1)} all-gather(bf16[1,48,1152]{2,1,0:T(8,128)(2,1)S(1)} %get-tuple-element.111), channel_id=4, replica_groups=mesh['fsdp'=8,'rep'=4] {'fsdp'}, dimensions={1}, use_global_device_ids=true | all-gather | bytes 995328 | tf_op jit(solution)/shard_map/all_gather | solution.py:251
  241.4 11.6 multiply_convert_fusion.3
  253.0 8.4 fusion.152
  295.2 11.1 multiply_convert_fusion.2
  306.4 14.5 %fusion.168 = (bf16[1536]{0:T(1024)(128)(2,1)}, bf16[8,256,1536]{2,1,0:T(8,128)(2,1)S(1)}) fusion(f32[8,256,1536]{2,1,0:T(8,128)} %get-tuple-element.146, f32[1536]{0:T(1024)} %convert_element_type.337, bf16[1,1536,384]{2,1,0:T(8,128)(2,1)} %all-gather.37.cloned.1.call-done, f32[8,256,384]{2,1,0:T(8,128)} %param.15, f32[8,384]{1,0:T(8,128)} %get-tuple-element.112), kind=kOutput, calls=%fused_computation.276 | convolution fusion | flops 2483550720 | bytes 23221248 | tf_op jit(solution)/shard_map/dot_general | solution.py:32
  327.4 9.0 multiply_reduce_fusion.23
  344.6 9.6 bitcast_convert_fusion.2
  360.5 22.9 %fusion.85 = bf16[8,6,64,256]{3,2,1,0:T(8,128)(2,1)} fusion(bf16[8,256,6,64]{1,3,2,0:T(8,128)(2,1)} %bitcast.264, f32[8,6,256,256]{2,3,1,0:T(8,128)} %fusion.170, f32[8,6,256,256]{2,3,1,0:T(8,128)} %copy-done.1, f32[8,6,256]{2,1,0:T(8,128)S(1)} %log_add_fusion), kind=kOutput, calls=%fused_computation.139 | convolution fusion | flops 431763712 | bytes 28360704 | tf_op jit(solution)/shard_map/bhqk,bqhe->bkhe/dot_general | solution.py:21
  383.4 21.4 %bitcast_convert_fusion.3 = (bf16[8,256,6,64]{1,3,2,0:T(8,128)(2,1)}, f32[8,6,64,256]{3,2,1,0:T(8,128)}) fusion(bf16[8,256,6,64]{1,3,2,0:T(8,128)(2,1)} %bitcast.262, f32[8,6,256,256]{2,3,1,0:T(8,128)} %fusion.170, f32[8,6,256,256]{2,3,1,0:T(8,128)} %copy-done.1, f32[8,6,256]{2,1,0:T(8,128)S(1)} %log_add_fusion), kind=kOutput, calls=%fused_computation.61 | convolution fusion | flops 431763712 | bytes 31506432 | tf_op jit(solution)/shard_map/bhqk,bkhe->bqhe/dot_general | solution.py:21
  419.7 7.3 multiply_reduce_fusion.11
  438.9 13.3 %fusion.169 = (bf16[1536]{0:T(1024)(128)(2,1)S(1)}, bf16[8,256,1536]{2,1,0:T(8,128)(2,1)S(1)}) fusion(f32[8,256,1536]{2,1,0:T(8,128)} %get-tuple-element.140, f32[1536]{0:T(1024)S(1)} %copy-done.79, bf16[1,1536,384]{2,1,0:T(8,128)(2,1)S(1)} %copy-done.97, f32[8,256,384]{2,1,0:T(8,128)S(1)} %get-tuple-element.85, f32[8,384]{1,0:T(8,128)S(1)} %get-tuple-element.120), kind=kOutput, calls=%fused_computation.277 | convolution fusion | flops 2483550720 | bytes 23221248 | tf_op jit(solution)/shard_map/dot_general | solution.py:32
  467.9 9.1 bitcast_convert_fusion
  486.1 22.5 %bitcast_convert_fusion.1 = (bf16[8,256,6,64]{1,3,2,0:T(8,128)(2,1)S(1)}, f32[8,6,64,256]{3,2,1,0:T(8,128)}) fusion(bf16[8,256,6,64]{1,3,2,0:T(8,128)(2,1)S(1)} %bitcast.260, f32[8,6,256,256]{2,3,1,0:T(8,128)} %fusion.171, f32[8,6,256,256]{2,3,1,0:T(8,128)} %copy-done, f32[8,6,256]{2,1,0:T(8,128)S(1)} %copy-done.32), kind=kOutput, calls=%fused_computation.57 | convolution fusion | flops 431763712 | bytes 31506432 | tf_op jit(solution)/shard_map/bhqk,bkhe->bqhe/dot_general | solution.py:21
  510.2 22.3 %fusion.82 = bf16[8,6,64,256]{3,2,1,0:T(8,128)(2,1)} fusion(bf16[8,256,6,64]{1,3,2,0:T(8,128)(2,1)S(1)} %bitcast.258, f32[8,6,256,256]{2,3,1,0:T(8,128)} %fusion.171, f32[8,6,256,256]{2,3,1,0:T(8,128)} %copy-done, f32[8,6,256]{2,1,0:T(8,128)S(1)} %copy-done.32), kind=kOutput, calls=%fused_computation.138 | convolution fusion | flops 431763712 | bytes 28360704 | tf_op jit(solution)/shard_map/bhqk,bqhe->bkhe/dot_general | solution.py:21
  542.0 7.5 fusion.69
  549.6 8.2 fusion.73
  558.0 8.2 fusion.72
  566.3 7.6 fusion.66
  598.4 33.9 %all-reduce.20 = (bf16[2304]{0:T(1024)(128)(2,1)S(1)}, bf16[2304]{0:T(1024)(128)(2,1)S(1)}, bf16[768]{0:T(1024)(128)(2,1)S(1)}, bf16[768]{0:T(1024)(128)(2,1)S(1...) all-reduce(bf16[2304]{0:T(1024)(128)(2,1)S(1)} %reduce_sum.477, ...), channel_id=25, replica_groups=mesh['fsdp'=8,'rep'=4] {'fsdp'}, use_global_device_ids=true, to_apply=%region_42.43.clone | all-reduce | flops 10752 | bytes 43008
  649.9 31.7 %reduce-scatter.15.cloned.1.call-done = bf16[48,1152]{1,0:T(8,128)(2,1)} async-done(((bf16[384,1152]{1,0:T(8,128)(2,1)}), bf16[48,1152]{1,0:T(8,128)(2,1)}) %reduce-scatter.15.cloned.1.call-update) | async-done | bytes 110608 | tf_op jit(solution)/shard_map/reduce_scatter | solution.py:278
  681.6 66.9 %reduce-scatter.25.cloned.1.call-done = bf16[48,1536]{1,0:T(8,128)(2,1)} async-done(((bf16[384,1536]{1,0:T(8,128)(2,1)}), bf16[48,1536]{1,0:T(8,128)(2,1)}) %reduce-scatter.25.cloned.1.call-update) | async-done | bytes 147472 | tf_op jit(solution)/shard_map/reduce_scatter | solution.py:290
  748.5 67.0 %reduce-scatter.29.cloned.1.call-done = bf16[192,384]{1,0:T(8,128)(2,1)} async-done(((bf16[1536,384]{1,0:T(8,128)(2,1)}), bf16[192,384]{1,0:T(8,128)(2,1)}) %reduce-scatter.29.cloned.1.call-update) | async-done | bytes 147472 | tf_op jit(solution)/shard_map/reduce_scatter | solution.py:296
  815.6 67.1 %reduce-scatter.27.cloned.1.call-done = bf16[192,384]{1,0:T(8,128)(2,1)} async-done(((bf16[1536,384]{1,0:T(8,128)(2,1)}), bf16[192,384]{1,0:T(8,128)(2,1)}) %reduce-scatter.27.cloned.1.call-update) | async-done | bytes 147472 | tf_op jit(solution)/shard_map/reduce_scatter | solution.py:296
  882.7 67.0 %reduce-scatter.23.cloned.1.call-done = bf16[48,1536]{1,0:T(8,128)(2,1)} async-done(((bf16[384,1536]{1,0:T(8,128)(2,1)}), bf16[48,1536]{1,0:T(8,128)(2,1)}) %reduce-scatter.23.cloned.1.call-update) | async-done | bytes 147472 | tf_op jit(solution)/shard_map/reduce_scatter | solution.py:290
  949.6 69.0 %reduce-scatter.13.cloned.1.call-done = bf16[48,2304]{1,0:T(8,128)(2,1)} async-done(((bf16[384,2304]{1,0:T(8,128)(2,1)}), bf16[48,2304]{1,0:T(8,128)(2,1)}) %reduce-scatter.13.cloned.1.call-update) | async-done | bytes 221200 | tf_op jit(solution)/shard_map/reduce_scatter | solution.py:272
  1018.6 68.8 %reduce-scatter.11.cloned.1.call-done = bf16[48,2304]{1,0:T(8,128)(2,1)} async-done(((bf16[384,2304]{1,0:T(8,128)(2,1)}), bf16[48,2304]{1,0:T(8,128)(2,1)}) %reduce-scatter.11.cloned.1.call-update) | async-done | bytes 221200 | tf_op jit(solution)/shard_map/reduce_scatter | solution.py:272
  1087.4 34.4 %all-reduce.27.cloned.1.call-done = (bf16[1,288]{1,0:T(2,128)(2,1)}, bf16[1,288]{1,0:T(2,128)(2,1)}, bf16[1,96]{1,0:T(2,128)(2,1)}, bf16[1,96]{1,0:T(2,128)(2,1)...) async-done(((bf16[1,288]{1,0:T(2,128)(2,1)}, ...) | async-done | bytes 76432 | tf_op jit(solution)/shard_map/psum | solution.py:305
  1129.4 35.8 %all-reduce.29.cloned.1.call-done = (bf16[1,48,2304]{2,1,0:T(8,128)(2,1)}, bf16[1,48,2304]{2,1,0:T(8,128)(2,1)}, bf16[1,48,1152]{2,1,0:T(8,128)(2,1)}, bf16[1,48...) async-done(((bf16[1,48,2304]{2,1,0:T(8,128)(2,1)}, ...) | async-done | bytes 1253392 | tf_op jit(solution)/shard_map/psum | solution.py:304
  (421 shorter events, 226.0 us)
Async XLA Ops:
  7.3 57.5 %copy-start.2 = (f32[8,256,384]{2,1,0:T(8,128)S(1)}, f32[8,256,384]{2,1,0:T(8,128)}, u32[]{:S(2)}) copy-start(f32[8,256,384]{2,1,0:T(8,128)} %param.13) | copy-start | bytes 9437188
  7.3 196.7 %all-gather.27.cloned.1.call-start = ((), (), s32[]{:S(2)}) async-start(), calls=%async_computation.20 | async-start | bytes 1990656 | tf_op jit(solution)/shard_map/all_gather | solution.py:251
  9.3 197.1 %all-gather.33.cloned.1.call-start = ((), (), s32[]{:S(2)}) async-start(), calls=%async_computation.23 | async-start | bytes 1990656 | tf_op jit(solution)/shard_map/all_gather | solution.py:251
  10.1 231.2 %all-gather.29.cloned.1.call-start = ((), (), s32[]{:S(2)}) async-start(), calls=%async_computation.21 | async-start | bytes 1327104 | tf_op jit(solution)/shard_map/all_gather | solution.py:251
  11.9 241.1 %all-gather.31.cloned.1.call-start = ((), (), s32[]{:S(2)}) async-start(), calls=%async_computation.22 | async-start | bytes 1327104 | tf_op jit(solution)/shard_map/all_gather | solution.py:251
  13.7 281.6 %all-gather.35.cloned.1.call-start = ((), (), s32[]{:S(2)}) async-start(), calls=%async_computation.24 | async-start | bytes 1327104 | tf_op jit(solution)/shard_map/all_gather | solution.py:251
  14.3 292.1 %all-gather.37.cloned.1.call-start = ((), (), s32[]{:S(2)}) async-start(), calls=%async_computation.25 | async-start | bytes 1327104 | tf_op jit(solution)/shard_map/all_gather | solution.py:251
  14.8 631.4 %reduce-scatter.21.cloned.1.call-start = ((), (), s32[]{:S(2)}) async-start(), calls=%async_computation.15 | async-start | bytes 331776 | tf_op jit(solution)/shard_map/reduce_scatter | solution.py:284
  18.2 188.2 %copy-start.36 = (bf16[8,384]{1,0:T(8,128)(2,1)}, bf16[8,384]{1,0:T(8,128)(2,1)S(1)}, u32[]{:S(2)}) copy-start(bf16[8,384]{1,0:T(8,128)(2,1)S(1)} %multiply_convert_fusion.12) | copy-start | bytes 18436
  65.2 143.7 %copy-start.40 = (f32[8,256]{1,0:T(8,128)}, f32[8,256]{1,0:T(8,128)S(1)}, u32[]{:S(2)}) copy-start(f32[8,256]{1,0:T(8,128)S(1)} %broadcast_multiply_fusion.11) | copy-start | bytes 24580
  65.2 138.1 %copy-start.71 = (bf16[1,768]{1,0:T(2,128)(2,1)S(1)}, bf16[1,768]{1,0:T(2,128)(2,1)}, u32[]{:S(2)}) copy-start(bf16[1,768]{1,0:T(2,128)(2,1)} %reshape.387) | copy-start | bytes 4612
  65.2 138.1 %copy-start.72 = (bf16[1,768]{1,0:T(2,128)(2,1)S(1)}, bf16[1,768]{1,0:T(2,128)(2,1)}, u32[]{:S(2)}) copy-start(bf16[1,768]{1,0:T(2,128)(2,1)} %reshape.402) | copy-start | bytes 4612
  100.4 108.5 %copy-start.53 = (f32[8,256]{1,0:T(8,128)S(1)}, f32[8,256]{1,0:T(8,128)}, u32[]{:S(2)}) copy-start(f32[8,256]{1,0:T(8,128)} %add_rsqrt_fusion.3) | copy-start | bytes 24580
  131.8 103.9 %copy-start.27 = (bf16[1,384,384]{2,1,0:T(8,128)(2,1)}, bf16[1,384,384]{2,1,0:T(8,128)(2,1)S(1)}, u32[]{:S(2)}) copy-start(bf16[1,384,384]{2,1,0:T(8,128)(2,1)S(1)} %all-gather.4) | copy-start | bytes 884740
  206.4 29.3 %copy-start.34 = (f32[8,384]{1,0:T(8,128)}, f32[8,384]{1,0:T(8,128)S(1)}, u32[]{:S(2)}) copy-start(f32[8,384]{1,0:T(8,128)S(1)} %get-tuple-element.125) | copy-start | bytes 36868
  206.4 34.9 %copy-start.45 = (f32[8,384]{1,0:T(8,128)}, f32[8,384]{1,0:T(8,128)S(1)}, u32[]{:S(2)}) copy-start(f32[8,384]{1,0:T(8,128)S(1)} %get-tuple-element.122) | copy-start | bytes 36868
  432.8 213.4 %reduce-scatter.19.cloned.1.call-start = ((), (), s32[]{:S(2)}) async-start(), calls=%async_computation.14 | async-start | bytes 331776 | tf_op jit(solution)/shard_map/reduce_scatter | solution.py:284
  438.8 18.0 %copy-start.19 = (f32[8,256,384]{2,1,0:T(8,128)}, f32[8,256,384]{2,1,0:T(8,128)S(1)}, u32[]{:S(2)}) copy-start(f32[8,256,384]{2,1,0:T(8,128)S(1)} %get-tuple-element.85) | copy-start | bytes 9437188
  467.6 182.3 %reduce-scatter.17.cloned.1.call-start = ((), (), s32[]{:S(2)}) async-start(), calls=%async_computation.13 | async-start | bytes 995328 | tf_op jit(solution)/shard_map/reduce_scatter | solution.py:278
  477.0 204.6 %reduce-scatter.15.cloned.1.call-start = ((), (), s32[]{:S(2)}) async-start(), calls=%async_computation.12 | async-start | bytes 995328 | tf_op jit(solution)/shard_map/reduce_scatter | solution.py:278
  510.2 25.1 %copy-start.41 = (f32[8,256]{1,0:T(8,128)S(1)}, f32[8,256]{1,0:T(8,128)}, u32[]{:S(2)}) copy-start(f32[8,256]{1,0:T(8,128)} %copy-done.40) | copy-start | bytes 24580
  510.2 25.1 %copy-start.44 = (f32[8,384]{1,0:T(8,128)S(1)}, f32[8,384]{1,0:T(8,128)}, u32[]{:S(2)}) copy-start(f32[8,384]{1,0:T(8,128)} %copy-done.43) | copy-start | bytes 36868
  510.2 25.1 %copy-start.54 = (f32[8,256]{1,0:T(8,128)S(1)}, f32[8,256]{1,0:T(8,128)}, u32[]{:S(2)}) copy-start(f32[8,256]{1,0:T(8,128)} %add_rsqrt_fusion.3) | copy-start | bytes 24580
  510.2 25.1 %copy-start.65 = (f32[8,384]{1,0:T(8,128)S(1)}, f32[8,384]{1,0:T(8,128)}, u32[]{:S(2)}) copy-start(f32[8,384]{1,0:T(8,128)} %copy-done.64) | copy-start | bytes 36868
  541.5 207.0 %reduce-scatter.25.cloned.1.call-start = ((), (), s32[]{:S(2)}) async-start(), calls=%async_computation.17 | async-start | bytes 1327104 | tf_op jit(solution)/shard_map/reduce_scatter | solution.py:290
  549.6 266.0 %reduce-scatter.29.cloned.1.call-start = ((), (), s32[]{:S(2)}) async-start(), calls=%async_computation.19 | async-start | bytes 1327104 | tf_op jit(solution)/shard_map/reduce_scatter | solution.py:296
  557.9 324.8 %reduce-scatter.27.cloned.1.call-start = ((), (), s32[]{:S(2)}) async-start(), calls=%async_computation.18 | async-start | bytes 1327104 | tf_op jit(solution)/shard_map/reduce_scatter | solution.py:296
  566.3 383.4 %reduce-scatter.23.cloned.1.call-start = ((), (), s32[]{:S(2)}) async-start(), calls=%async_computation.16 | async-start | bytes 1327104 | tf_op jit(solution)/shard_map/reduce_scatter | solution.py:290
  573.9 444.7 %reduce-scatter.13.cloned.1.call-start = ((), (), s32[]{:S(2)}) async-start(), calls=%async_computation.11 | async-start | bytes 1990656 | tf_op jit(solution)/shard_map/reduce_scatter | solution.py:272
  577.1 510.3 %reduce-scatter.11.cloned.1.call-start = ((), (), s32[]{:S(2)}) async-start(), calls=%async_computation.10 | async-start | bytes 1990656 | tf_op jit(solution)/shard_map/reduce_scatter | solution.py:272
  586.7 535.1 %all-reduce.27.cloned.1.call-start = ((), (), s32[]{:S(2)}) async-start(), calls=%async_computation.26 | async-start | bytes 163840 | tf_op jit(solution)/shard_map/psum | solution.py:305
  646.2 519.0 %all-reduce.29.cloned.1.call-start = ((), (), s32[]{:S(2)}) async-start(), calls=%async_computation.27 | async-start | bytes 2506752 | tf_op jit(solution)/shard_map/psum | solution.py:304
  (88 other events, 572.6 us)
Sparse Core Ops, SparseCore 0:
  10.8 49.4 all-gather.26
  63.0 47.2 all-gather.32
  113.1 45.0 all-gather.28
  160.2 43.9 all-gather.30
  206.8 39.9 all-gather.34
  248.8 39.7 all-gather.36
  432.9 56.9 reduce-scatter.20
  493.7 58.5 reduce-scatter.18
  556.3 61.1 reduce-scatter.16
  620.7 60.8 reduce-scatter.14
  685.0 63.4 reduce-scatter.24
  751.8 63.7 reduce-scatter.28
  818.9 63.6 reduce-scatter.26
  885.9 63.6 reduce-scatter.22
  952.9 65.6 reduce-scatter.12
  1021.9 65.4 reduce-scatter.10
  1091.6 30.2 all-reduce.26
  1124.6 40.5 all-reduce.28
where the time goes:
time: 1190 us; the launch traced here: 1180 us
  waiting for transfers between devices  510 us (43%)
  matrix products  311 us (26%)
  blocking collectives  210 us (18%)
  local copies, waits for them, and re-layouts  74.5 us (6%)
  other arithmetic  51.7 us (4%)
  between operations  21.2 us (2%)
    reduce_scatter x2, waiting for transfers between devices, body(): lax.psum_scatter(gradients[0].astype(jnp.bfloat16), 'fsdp', scatter_dimen...  138 us
    all_gather x4, blocking collectives, body(): lax.all_gather(as_sent(owned_rows), 'fsdp', axis=0, tiled=True)  137 us
    dot_general x12, matrix products, pair_product(): return jnp.einsum(form, left, right, preferred_element_type=jnp.float32)  136 us
    reduce_scatter x2, waiting for transfers between devices, body(): lax.psum_scatter(gradients[8].astype(jnp.bfloat16), 'fsdp', scatter_dimen...  134 us
    reduce_scatter x2, waiting for transfers between devices, body(): lax.psum_scatter(gradients[6].astype(jnp.bfloat16), 'fsdp', scatter_dimen...  134 us
    unnamed x2, blocking collectives  73.5 us
    dot_general x8, matrix products, matmul_back(): lax.dot_general(flattened, weight, (((1,), (1,)), ((), ())), preferred_el...  55.6 us
    dot_general x8, matrix products, matmul(): result = jnp.dot(flattened, weight, preferred_element_type=jnp.float32)  53.9 us
  transfers between devices with their start and end apart: 18, of which 9 were waited for; matrix products, arithmetic and copies ran while one was open for 25% of the time, Pallas kernels for 0%

commit v1 on v0

--- a/solution.py
+++ b/solution.py
@@ -302,7 +302,9 @@
         )
         owned_sums = (
             lax.psum(owned_sums[0].astype(jnp.bfloat16), "rep").astype(jnp.float32),
-            lax.psum(owned_sums[1].astype(jnp.bfloat16), "rep").astype(jnp.float32),
+            jnp.sum(lax.all_gather(owned_sums[1].astype(jnp.bfloat16), "rep"), axis=0).astype(
+                jnp.float32
+            ),
             lax.psum(owned_sums[2].astype(jnp.bfloat16), "rep").astype(jnp.float32),
             lax.psum(owned_sums[3].astype(jnp.bfloat16), "rep").astype(jnp.float32),
             lax.psum(owned_sums[4].astype(jnp.bfloat16), "rep").astype(jnp.float32),

time: 1190 us -> 1270 us (1.067)
  waiting for transfers between devices: 510 us -> 597 us
    reduce_scatter x2, waiting for transfers between devices: 31.7 us -> 102 us  [body(): lax.psum_scatter(gradients[2].astype(jnp.bfloat16), 'fsdp', scatter_dimen...]
    reduce_scatter x2, waiting for transfers between devices: 0.01 us -> 53.6 us  [body(): lax.psum_scatter(gradients[4].astype(jnp.bfloat16), 'fsdp', scatter_dimen...]
    psum x1 -> x0, waiting for transfers between devices: 34.4 us -> none  [body(): lax.psum(owned_sums[1].astype(jnp.bfloat16), 'rep').astype(jnp.float32)]
  transfers between devices with their start and end apart: 18 -> 18, of which waited for: 9 -> 10; matrix products, arithmetic and copies ran while one was open for 25% -> 16% of each run, Pallas kernels for 0% -> 0%
where the time goes in v1:
time: 1270 us; the launch traced here: 1260 us
  waiting for transfers between devices  597 us (47%)
  matrix products  313 us (25%)
  blocking collectives  209 us (16%)
  local copies, waits for them, and re-layouts  77.9 us (6%)
  other arithmetic  43.9 us (3%)
  between operations  22 us (2%)
    reduce_scatter x2, waiting for transfers between devices, body(): lax.psum_scatter(gradients[0].astype(jnp.bfloat16), 'fsdp', scatter_dimen...  138 us
    dot_general x12, matrix products, pair_product(): return jnp.einsum(form, left, right, preferred_element_type=jnp.float32)  137 us
    all_gather x4, blocking collectives, body(): lax.all_gather(as_sent(owned_rows), 'fsdp', axis=0, tiled=True)  136 us
    reduce_scatter x2, waiting for transfers between devices, body(): lax.psum_scatter(gradients[8].astype(jnp.bfloat16), 'fsdp', scatter_dimen...  134 us
    reduce_scatter x2, waiting for transfers between devices, body(): lax.psum_scatter(gradients[6].astype(jnp.bfloat16), 'fsdp', scatter_dimen...  134 us
    reduce_scatter x2, waiting for transfers between devices, body(): lax.psum_scatter(gradients[2].astype(jnp.bfloat16), 'fsdp', scatter_dimen...  102 us
    unnamed x2, blocking collectives  73.5 us
    dot_general x8, matrix products, matmul_back(): lax.dot_general(flattened, weight, (((1,), (1,)), ((), ())), preferred_el...  56.2 us
  transfers between devices with their start and end apart: 18, of which 10 were waited for; matrix products, arithmetic and copies ran while one was open for 16% of the time, Pallas kernels for 0%

profile of v1, /device:TPU:0, one launch (start us, length us, event | category | flops | bytes accessed | tf_op | source)
XLA Modules:
  0.0 1263.8 jit_solution(17372484262797782632)
XLA Ops:
  24.4 39.7 %all-reduce.23 = (bf16[768]{0:T(1024)(128)(2,1)S(1)}, bf16[2304]{0:T(1024)(128)(2,1)S(1)}, bf16[384]{0:T(512)(128)(2,1)S(1)}, bf16[1536]{0:T(1024)(128)(2,1)S(1)...) all-reduce(bf16[768]{0:T(1024)(128)(2,1)S(1)} %dynamic-update-slice, ...), channel_id=5, replica_groups=mesh['fsdp'=8,'rep'=4] {'fsdp'}, use_global_device_ids=true, to_apply=%add.1 | all-reduce | flops 10752 | bytes 43008
  69.9 33.5 %all-gather.14 = bf16[1,384,384]{2,1,0:T(8,128)(2,1)} all-gather(bf16[1,48,384]{2,1,0:T(8,128)(2,1)S(1)} %get-tuple-element.118), channel_id=16, replica_groups=mesh['fsdp'=8,'rep'=4] {'fsdp'}, dimensions={1}, use_global_device_ids=true | all-gather | bytes 331776 | tf_op jit(solution)/shard_map/all_gather | solution.py:251
  103.4 31.3 %all-gather.4 = bf16[1,384,384]{2,1,0:T(8,128)(2,1)S(1)} all-gather(bf16[1,48,384]{2,1,0:T(8,128)(2,1)S(1)} %get-tuple-element.119), channel_id=6, replica_groups=mesh['fsdp'=8,'rep'=4] {'fsdp'}, dimensions={1}, use_global_device_ids=true | all-gather | bytes 331776 | tf_op jit(solution)/shard_map/all_gather | solution.py:251
  134.7 35.5 %all-gather.12 = bf16[1,384,1152]{2,1,0:T(8,128)(2,1)} all-gather(bf16[1,48,1152]{2,1,0:T(8,128)(2,1)S(1)} %get-tuple-element.110), channel_id=14, replica_groups=mesh['fsdp'=8,'rep'=4] {'fsdp'}, dimensions={1}, use_global_device_ids=true | all-gather | bytes 995328 | tf_op jit(solution)/shard_map/all_gather | solution.py:251
  170.2 35.3 %all-gather.2 = bf16[1,384,1152]{2,1,0:T(8,128)(2,1)} all-gather(bf16[1,48,1152]{2,1,0:T(8,128)(2,1)S(1)} %get-tuple-element.111), channel_id=4, replica_groups=mesh['fsdp'=8,'rep'=4] {'fsdp'}, dimensions={1}, use_global_device_ids=true | all-gather | bytes 995328 | tf_op jit(solution)/shard_map/all_gather | solution.py:251
  243.8 11.5 multiply_convert_fusion.3
  255.4 8.5 fusion.152
  297.5 11.1 multiply_convert_fusion.2
  308.6 14.8 %fusion.168 = (bf16[1536]{0:T(1024)(128)(2,1)}, bf16[8,256,1536]{2,1,0:T(8,128)(2,1)S(1)}) fusion(f32[8,256,1536]{2,1,0:T(8,128)} %get-tuple-element.146, f32[1536]{0:T(1024)} %convert_element_type.363, bf16[1,1536,384]{2,1,0:T(8,128)(2,1)} %all-gather.39.cloned.1.call-done, f32[8,256,384]{2,1,0:T(8,128)} %param.15, f32[8,384]{1,0:T(8,128)} %get-tuple-element.112), kind=kOutput, calls=%fused_computation.276 | convolution fusion | flops 2483550720 | bytes 23221248 | tf_op jit(solution)/shard_map/dot_general | solution.py:32
  330.0 9.0 multiply_reduce_fusion.23
  347.1 9.6 bitcast_convert_fusion.2
  363.0 22.9 %fusion.85 = bf16[8,6,64,256]{3,2,1,0:T(8,128)(2,1)} fusion(bf16[8,256,6,64]{1,3,2,0:T(8,128)(2,1)} %bitcast.265, f32[8,6,256,256]{2,3,1,0:T(8,128)} %fusion.170, f32[8,6,256,256]{2,3,1,0:T(8,128)} %copy-done.1, f32[8,6,256]{2,1,0:T(8,128)S(1)} %log_add_fusion), kind=kOutput, calls=%fused_computation.139 | convolution fusion | flops 431763712 | bytes 28360704 | tf_op jit(solution)/shard_map/bhqk,bqhe->bkhe/dot_general | solution.py:21
  385.9 21.4 %bitcast_convert_fusion.3 = (bf16[8,256,6,64]{1,3,2,0:T(8,128)(2,1)}, f32[8,6,64,256]{3,2,1,0:T(8,128)}) fusion(bf16[8,256,6,64]{1,3,2,0:T(8,128)(2,1)} %bitcast.263, f32[8,6,256,256]{2,3,1,0:T(8,128)} %fusion.170, f32[8,6,256,256]{2,3,1,0:T(8,128)} %copy-done.1, f32[8,6,256]{2,1,0:T(8,128)S(1)} %log_add_fusion), kind=kOutput, calls=%fused_computation.61 | convolution fusion | flops 431763712 | bytes 31506432 | tf_op jit(solution)/shard_map/bhqk,bkhe->bqhe/dot_general | solution.py:21
  425.3 13.9 %fusion.169 = (bf16[1536]{0:T(1024)(128)(2,1)}, bf16[8,256,1536]{2,1,0:T(8,128)(2,1)S(1)}) fusion(f32[8,256,1536]{2,1,0:T(8,128)} %get-tuple-element.140, f32[1536]{0:T(1024)S(1)} %copy-done.88, bf16[1,1536,384]{2,1,0:T(8,128)(2,1)S(1)} %copy-done.110, f32[8,256,384]{2,1,0:T(8,128)S(1)} %get-tuple-element.85, f32[8,384]{1,0:T(8,128)S(1)} %copy-done.52), kind=kOutput, calls=%fused_computation.277 | convolution fusion | flops 2483550720 | bytes 23221248 | tf_op jit(solution)/shard_map/dot_general | solution.py:32
  451.8 9.3 bitcast_convert_fusion
  467.4 22.8 %fusion.82 = bf16[8,6,64,256]{3,2,1,0:T(8,128)(2,1)} fusion(bf16[8,256,6,64]{1,3,2,0:T(8,128)(2,1)} %bitcast.261, f32[8,6,256,256]{2,3,1,0:T(8,128)} %fusion.171, f32[8,6,256,256]{2,3,1,0:T(8,128)} %copy-done, f32[8,6,256]{2,1,0:T(8,128)S(1)} %copy-done.40), kind=kOutput, calls=%fused_computation.138 | convolution fusion | flops 431763712 | bytes 28360704 | tf_op jit(solution)/shard_map/bhqk,bqhe->bkhe/dot_general | solution.py:21
  490.2 22.8 %bitcast_convert_fusion.1 = (bf16[8,256,6,64]{1,3,2,0:T(8,128)(2,1)}, f32[8,6,64,256]{3,2,1,0:T(8,128)}) fusion(bf16[8,256,6,64]{1,3,2,0:T(8,128)(2,1)S(1)} %bitcast.259, f32[8,6,256,256]{2,3,1,0:T(8,128)} %fusion.171, f32[8,6,256,256]{2,3,1,0:T(8,128)} %copy-done, f32[8,6,256]{2,1,0:T(8,128)S(1)} %copy-done.40), kind=kOutput, calls=%fused_computation.57 | convolution fusion | flops 431763712 | bytes 31506432 | tf_op jit(solution)/shard_map/bhqk,bkhe->bqhe/dot_general | solution.py:21
  543.1 33.9 %all-reduce.22 = (bf16[2304]{0:T(1024)(128)(2,1)S(1)}, bf16[2304]{0:T(1024)(128)(2,1)S(1)}, bf16[768]{0:T(1024)(128)(2,1)S(1)}, bf16[768]{0:T(1024)(128)(2,1)S(1...) all-reduce(bf16[2304]{0:T(1024)(128)(2,1)S(1)} %reduce_sum.502, ...), channel_id=27, replica_groups=mesh['fsdp'=8,'rep'=4] {'fsdp'}, use_global_device_ids=true, to_apply=%region_42.43.clone | all-reduce | flops 10752 | bytes 43008
  582.5 53.6 %reduce-scatter.19.cloned.1.call-done = bf16[48,384]{1,0:T(8,128)(2,1)} async-done(((bf16[384,384]{1,0:T(8,128)(2,1)}), bf16[48,384]{1,0:T(8,128)(2,1)}) %reduce-scatter.19.cloned.1.call-update) | async-done | bytes 36880 | tf_op jit(solution)/shard_map/reduce_scatter | solution.py:284
  649.5 7.6 fusion.69
  657.1 8.2 fusion.73
  665.4 8.3 fusion.72
  673.8 7.6 fusion.66
  700.9 37.4 %reduce-scatter.17.cloned.1.call-done = bf16[48,1152]{1,0:T(8,128)(2,1)} async-done(((bf16[384,1152]{1,0:T(8,128)(2,1)}), bf16[48,1152]{1,0:T(8,128)(2,1)}) %reduce-scatter.17.cloned.1.call-update) | async-done | bytes 110608 | tf_op jit(solution)/shard_map/reduce_scatter | solution.py:278
  738.3 64.4 %reduce-scatter.15.cloned.1.call-done = bf16[48,1152]{1,0:T(8,128)(2,1)} async-done(((bf16[384,1152]{1,0:T(8,128)(2,1)}), bf16[48,1152]{1,0:T(8,128)(2,1)}) %reduce-scatter.15.cloned.1.call-update) | async-done | bytes 110608 | tf_op jit(solution)/shard_map/reduce_scatter | solution.py:278
  802.7 66.7 %reduce-scatter.25.cloned.1.call-done = bf16[48,1536]{1,0:T(8,128)(2,1)} async-done(((bf16[384,1536]{1,0:T(8,128)(2,1)}), bf16[48,1536]{1,0:T(8,128)(2,1)}) %reduce-scatter.25.cloned.1.call-update) | async-done | bytes 147472 | tf_op jit(solution)/shard_map/reduce_scatter | solution.py:290
  869.5 67.1 %reduce-scatter.29.cloned.1.call-done = bf16[192,384]{1,0:T(8,128)(2,1)} async-done(((bf16[1536,384]{1,0:T(8,128)(2,1)}), bf16[192,384]{1,0:T(8,128)(2,1)}) %reduce-scatter.29.cloned.1.call-update) | async-done | bytes 147472 | tf_op jit(solution)/shard_map/reduce_scatter | solution.py:296
  936.6 67.0 %reduce-scatter.27.cloned.1.call-done = bf16[192,384]{1,0:T(8,128)(2,1)} async-done(((bf16[1536,384]{1,0:T(8,128)(2,1)}), bf16[192,384]{1,0:T(8,128)(2,1)}) %reduce-scatter.27.cloned.1.call-update) | async-done | bytes 147472 | tf_op jit(solution)/shard_map/reduce_scatter | solution.py:296
  1003.5 67.0 %reduce-scatter.23.cloned.1.call-done = bf16[48,1536]{1,0:T(8,128)(2,1)} async-done(((bf16[384,1536]{1,0:T(8,128)(2,1)}), bf16[48,1536]{1,0:T(8,128)(2,1)}) %reduce-scatter.23.cloned.1.call-update) | async-done | bytes 147472 | tf_op jit(solution)/shard_map/reduce_scatter | solution.py:290
  1070.5 69.3 %reduce-scatter.13.cloned.1.call-done = bf16[48,2304]{1,0:T(8,128)(2,1)} async-done(((bf16[384,2304]{1,0:T(8,128)(2,1)}), bf16[48,2304]{1,0:T(8,128)(2,1)}) %reduce-scatter.13.cloned.1.call-update) | async-done | bytes 221200 | tf_op jit(solution)/shard_map/reduce_scatter | solution.py:272
  1139.8 68.8 %reduce-scatter.11.cloned.1.call-done = bf16[48,2304]{1,0:T(8,128)(2,1)} async-done(((bf16[384,2304]{1,0:T(8,128)(2,1)}), bf16[48,2304]{1,0:T(8,128)(2,1)}) %reduce-scatter.11.cloned.1.call-update) | async-done | bytes 221200 | tf_op jit(solution)/shard_map/reduce_scatter | solution.py:272
  1215.6 33.7 %all-reduce.31.cloned.1.call-done = (bf16[1,48,2304]{2,1,0:T(8,128)(2,1)}, bf16[1,48,2304]{2,1,0:T(8,128)(2,1)}, bf16[1,48,1152]{2,1,0:T(8,128)(2,1)}, bf16[1,48...) async-done(((bf16[1,48,2304]{2,1,0:T(8,128)(2,1)}, ...) | async-done | bytes 1253392 | tf_op jit(solution)/shard_map/psum | solution.py:304
  (458 shorter events, 228.6 us)
Async XLA Ops:
  7.3 60.9 %copy-start.2 = (f32[8,256,384]{2,1,0:T(8,128)S(1)}, f32[8,256,384]{2,1,0:T(8,128)}, u32[]{:S(2)}) copy-start(f32[8,256,384]{2,1,0:T(8,128)} %param.13) | copy-start | bytes 9437188
  7.3 198.8 %all-gather.29.cloned.1.call-start = ((), (), s32[]{:S(2)}) async-start(), calls=%async_computation.20 | async-start | bytes 1990656 | tf_op jit(solution)/shard_map/all_gather | solution.py:251
  9.3 199.2 %all-gather.35.cloned.1.call-start = ((), (), s32[]{:S(2)}) async-start(), calls=%async_computation.23 | async-start | bytes 1990656 | tf_op jit(solution)/shard_map/all_gather | solution.py:251
  10.1 233.7 %all-gather.31.cloned.1.call-start = ((), (), s32[]{:S(2)}) async-start(), calls=%async_computation.21 | async-start | bytes 1327104 | tf_op jit(solution)/shard_map/all_gather | solution.py:251
  11.9 243.5 %all-gather.33.cloned.1.call-start = ((), (), s32[]{:S(2)}) async-start(), calls=%async_computation.22 | async-start | bytes 1327104 | tf_op jit(solution)/shard_map/all_gather | solution.py:251
  13.7 283.8 %all-gather.37.cloned.1.call-start = ((), (), s32[]{:S(2)}) async-start(), calls=%async_computation.24 | async-start | bytes 1327104 | tf_op jit(solution)/shard_map/all_gather | solution.py:251
  14.3 294.3 %all-gather.39.cloned.1.call-start = ((), (), s32[]{:S(2)}) async-start(), calls=%async_computation.25 | async-start | bytes 1327104 | tf_op jit(solution)/shard_map/all_gather | solution.py:251
  14.9 567.7 %reduce-scatter.21.cloned.1.call-start = ((), (), s32[]{:S(2)}) async-start(), calls=%async_computation.15 | async-start | bytes 331776 | tf_op jit(solution)/shard_map/reduce_scatter | solution.py:284
  22.1 186.4 %copy-start.44 = (bf16[8,384]{1,0:T(8,128)(2,1)}, bf16[8,384]{1,0:T(8,128)(2,1)S(1)}, u32[]{:S(2)}) copy-start(bf16[8,384]{1,0:T(8,128)(2,1)S(1)} %multiply_convert_fusion.12) | copy-start | bytes 18436
  68.5 142.5 %copy-start.46 = (f32[8,256]{1,0:T(8,128)}, f32[8,256]{1,0:T(8,128)S(1)}, u32[]{:S(2)}) copy-start(f32[8,256]{1,0:T(8,128)S(1)} %broadcast_multiply_fusion.11) | copy-start | bytes 24580
  68.5 136.9 %copy-start.80 = (bf16[1,768]{1,0:T(2,128)(2,1)S(1)}, bf16[1,768]{1,0:T(2,128)(2,1)}, u32[]{:S(2)}) copy-start(bf16[1,768]{1,0:T(2,128)(2,1)} %reshape.422) | copy-start | bytes 4612
  69.2 141.8 %copy-start.60 = (f32[8,256]{1,0:T(8,128)}, f32[8,256]{1,0:T(8,128)S(1)}, u32[]{:S(2)}) copy-start(f32[8,256]{1,0:T(8,128)S(1)} %add_rsqrt_fusion.3) | copy-start | bytes 24580
  69.9 138.7 %copy-start.57 = (f32[2304]{0:T(1024)S(1)}, f32[2304]{0:T(1024)}, u32[]{:S(2)}) copy-start(f32[2304]{0:T(1024)} %convert_element_type.361) | copy-start | bytes 27652
  134.7 103.5 %copy-start.33 = (bf16[1,384,384]{2,1,0:T(8,128)(2,1)}, bf16[1,384,384]{2,1,0:T(8,128)(2,1)S(1)}, u32[]{:S(2)}) copy-start(bf16[1,384,384]{2,1,0:T(8,128)(2,1)S(1)} %all-gather.4) | copy-start | bytes 884740
  208.5 29.7 %copy-start.42 = (f32[8,384]{1,0:T(8,128)}, f32[8,384]{1,0:T(8,128)S(1)}, u32[]{:S(2)}) copy-start(f32[8,384]{1,0:T(8,128)S(1)} %get-tuple-element.125) | copy-start | bytes 36868
  208.5 46.8 %copy-start.51 = (f32[8,384]{1,0:T(8,128)}, f32[8,384]{1,0:T(8,128)S(1)}, u32[]{:S(2)}) copy-start(f32[8,384]{1,0:T(8,128)S(1)} %get-tuple-element.120) | copy-start | bytes 36868
  211.0 53.6 %copy-start.53 = (f32[8,384]{1,0:T(8,128)}, f32[8,384]{1,0:T(8,128)S(1)}, u32[]{:S(2)}) copy-start(f32[8,384]{1,0:T(8,128)S(1)} %get-tuple-element.116) | copy-start | bytes 36868
  490.2 22.9 %copy-start.15 = (bf16[8,6,64,256]{3,2,1,0:T(8,128)(2,1)S(1)}, bf16[8,6,64,256]{3,2,1,0:T(8,128)(2,1)}, u32[]{:S(2)}) copy-start(bf16[8,6,64,256]{3,2,1,0:T(8,128)(2,1)} %copy-done.14) | copy-start | bytes 4718596
  516.2 119.9 %reduce-scatter.19.cloned.1.call-start = ((), (), s32[]{:S(2)}) async-start(), calls=%async_computation.14 | async-start | bytes 331776 | tf_op jit(solution)/shard_map/reduce_scatter | solution.py:284
  539.1 97.0 %copy-start.79 = (f32[8,384]{1,0:T(8,128)S(1)}, f32[8,384]{1,0:T(8,128)}, u32[]{:S(2)}) copy-start(f32[8,384]{1,0:T(8,128)} %get-tuple-element.115) | copy-start | bytes 36868
  543.0 156.3 %all-reduce.29.cloned.1.call-start = ((), (), s32[]{:S(2)}) async-start(), calls=%async_computation.26 | async-start | bytes 174080
  579.3 56.8 %copy-start.68 = (bf16[1152]{0:T(1024)(128)(2,1)}, bf16[1152]{0:T(1024)(128)(2,1)S(1)}, u32[]{:S(2)}) copy-start(bf16[1152]{0:T(1024)(128)(2,1)S(1)} %dynamic-update-slice.10) | copy-start | bytes 6916
  579.5 56.6 %copy-start.67 = (bf16[1152]{0:T(1024)(128)(2,1)}, bf16[1152]{0:T(1024)(128)(2,1)S(1)}, u32[]{:S(2)}) copy-start(bf16[1152]{0:T(1024)(128)(2,1)S(1)} %dynamic-update-slice.11) | copy-start | bytes 6916
  636.1 102.2 %reduce-scatter.17.cloned.1.call-start = ((), (), s32[]{:S(2)}) async-start(), calls=%async_computation.13 | async-start | bytes 995328 | tf_op jit(solution)/shard_map/reduce_scatter | solution.py:278
  642.9 159.8 %reduce-scatter.15.cloned.1.call-start = ((), (), s32[]{:S(2)}) async-start(), calls=%async_computation.12 | async-start | bytes 995328 | tf_op jit(solution)/shard_map/reduce_scatter | solution.py:278
  649.4 220.1 %reduce-scatter.25.cloned.1.call-start = ((), (), s32[]{:S(2)}) async-start(), calls=%async_computation.17 | async-start | bytes 1327104 | tf_op jit(solution)/shard_map/reduce_scatter | solution.py:290
  657.1 279.5 %reduce-scatter.29.cloned.1.call-start = ((), (), s32[]{:S(2)}) async-start(), calls=%async_computation.19 | async-start | bytes 1327104 | tf_op jit(solution)/shard_map/reduce_scatter | solution.py:296
  665.4 338.2 %reduce-scatter.27.cloned.1.call-start = ((), (), s32[]{:S(2)}) async-start(), calls=%async_computation.18 | async-start | bytes 1327104 | tf_op jit(solution)/shard_map/reduce_scatter | solution.py:296
  673.7 396.8 %reduce-scatter.23.cloned.1.call-start = ((), (), s32[]{:S(2)}) async-start(), calls=%async_computation.16 | async-start | bytes 1327104 | tf_op jit(solution)/shard_map/reduce_scatter | solution.py:290
  681.4 458.5 %reduce-scatter.13.cloned.1.call-start = ((), (), s32[]{:S(2)}) async-start(), calls=%async_computation.11 | async-start | bytes 1990656 | tf_op jit(solution)/shard_map/reduce_scatter | solution.py:272
  684.5 524.1 %reduce-scatter.11.cloned.1.call-start = ((), (), s32[]{:S(2)}) async-start(), calls=%async_computation.10 | async-start | bytes 1990656 | tf_op jit(solution)/shard_map/reduce_scatter | solution.py:272
  687.4 561.9 %all-reduce.31.cloned.1.call-start = ((), (), s32[]{:S(2)}) async-start(), calls=%async_computation.27 | async-start | bytes 2506752 | tf_op jit(solution)/shard_map/psum | solution.py:304
  (102 other events, 665.6 us)
Sparse Core Ops, SparseCore 0:
  10.8 48.9 all-gather.28
  62.6 47.1 all-gather.34
  112.6 45.6 all-gather.30
  160.3 44.6 all-gather.32
  207.6 39.5 all-gather.36
  249.3 39.7 all-gather.38
  516.3 57.1 reduce-scatter.20
  577.4 58.6 reduce-scatter.18
  640.5 31.1 all-reduce.28
  675.4 62.8 reduce-scatter.16
  741.7 60.9 reduce-scatter.14
  806.0 63.4 reduce-scatter.24
  872.9 63.6 reduce-scatter.28
  939.8 63.7 reduce-scatter.26
  1006.8 63.6 reduce-scatter.22
  1073.8 65.9 reduce-scatter.12
  1143.1 65.4 reduce-scatter.10
  1211.4 37.8 all-reduce.30
